TPU v7x, 128 devices: a whole 4x4x4 slice. The times are simulated.
128 devices in a mesh: seq: 64 (over y, x_hi, z, core), dp: 2 (over x_lo).
Axes of the slice: x: 4 (x_hi: 2, x_lo: 2; x = x_hi * 2 + x_lo), y: 4, z: 4, core: 2. Of those that a mesh axis runs over, the one named last changes fastest.
Arguments:
- acceptors: bfloat16 [2, 8192, 2560], P('dp', 'seq'), may hold values from -2 to 2
- lookups: bfloat16 [2, 8192, 2560], P('dp', 'seq'), may hold values from -0.3125 to 0.3125
- payloads: bfloat16 [2, 8192, 2560], P('dp', 'seq'), may hold values from -6 to 6
- lagged_fading_source: bfloat16 [2, 8192, 2560], P('dp', 'seq'), may hold values from -6 to 6
- response_cotangent: bfloat16 [2, 8192, 2560], P('dp', 'seq'), may hold values from -2.5 to 2.5
- fading_lowering_array: bfloat16 [2560, 128], replicated, may hold values from -0.125 to 0.125
- fading_raising_array: bfloat16 [2560, 128], replicated, may hold values from -1.25 to 1.25
- feature_fading_speed: float32 [2560], replicated, may hold values from 5.812872e-06 to 0.125
- present_reward: float32 [2560], replicated, may hold values from 2.828427 to 22.627417
Outputs:
- mixed: bfloat16 [2, 8192, 2560], P('dp', 'seq')
- grad_receptance: bfloat16 [2, 8192, 2560], P('dp', 'seq')
- lookup_deriv: bfloat16 [2, 8192, 2560], P('dp', 'seq')
- payload_deriv: bfloat16 [2, 8192, 2560], P('dp', 'seq')
- grad_decay_input: bfloat16 [2, 8192, 2560], P('dp', 'seq')
- grad_lora_a: float32 [2560, 128], P('dp')
- grad_lora_b: float32 [2560, 128], P('dp')
- grad_time_decay: float32 [2560], P('dp')
- present_reward_deriv: float32 [2560], P('dp')
All inputs are finite; a program needn't handle non-finite values.
Results may differ from a plain program's by a relative error of at most 0.006.
Values sent between devices are 32-bit elements.
A program may use at most 320 MiB of HBM per device.

v0:
```python
import jax
import jax.numpy as jnp
from jax import lax
from jax.experimental import pallas as pl
from jax.experimental.pallas import tpu as pltpu
from jax.sharding import PartitionSpec as P

F32 = jnp.float32
BF16 = jnp.bfloat16
TOK = 128
HALF = 64
GROUPS = 4
PAIRS = 5
WIDTH = PAIRS * 128
CHIPS = 32
CHUNKS = 2 * CHIPS
BATCH = CHUNKS // GROUPS
NN = (((1,), (0,)), ((), ()))
NT = (((1,), (1,)), ((), ()))
TN = (((0,), (0,)), ((), ()))


def dot(a, b, dims):
    return lax.dot_general(a, b, dims, preferred_element_type=F32)


def split(x, parts):
    pieces = []
    for _ in range(parts - 1):
        head = x.astype(BF16)
        pieces.append(head)
        x = x - head.astype(F32)
    pieces.append(x.astype(BF16))
    return pieces


def summed_by(matrix, x, parts):
    total = None
    for piece in split(x, parts):
        term = dot(matrix, piece, NN)
        total = term if total is None else total + term
    return total


def grids():
    row = lax.broadcasted_iota(jnp.int32, (TOK, TOK), 0)
    col = lax.broadcasted_iota(jnp.int32, (TOK, TOK), 1)
    same = (row < HALF) == (col < HALF)
    return row, col, same


def as_matrix(condition):
    return jnp.where(condition, 1.0, 0.0).astype(BF16)


def decay_sums(gate, raising, speed, lower):
    rank = dot(gate, raising, NT)
    log_decay = -speed * jnp.exp(rank)
    inclusive = summed_by(lower, log_decay, 3)
    return (
        log_decay,
        inclusive,
        inclusive - log_decay,
        inclusive[HALF - 1 : HALF],
        inclusive[TOK - 1 : TOK],
    )


def both(lhs, first, last, dims):
    return jnp.concatenate([dot(lhs[:HALF], first, dims), dot(lhs[HALF:], last, dims)], axis=0)


def packed(product, left):
    return jnp.where(left[:HALF], product[:HALF], product[HALF:])


def spread(state, left):
    zero = jnp.zeros_like(state)
    return jnp.concatenate(
        [jnp.where(left[:HALF], state, zero), jnp.where(left[:HALF], zero, state)], axis=0
    )


def whole_kernel(
    x_hbm, a_hbm, r_hbm, k_hbm, v_hbm, g_hbm, b_hbm, speed_ref, reward_ref,
    mixed_ref, dr_ref, dk_ref, dv_ref, dx_ref, red_ref,
    x_ref, a_ref, r_ref, k_ref, v_ref, g_ref, b_ref, fetch_sem,
    s0_ref, s1_ref, e0_ref, e1_ref,
    smooth_ref, gate_ref, log_ref, sum_ref, enter_ref, leave_ref, reached_ref, faded_ref,
    own_ref, pull_ref, ends_ref,
    mixed_near, dv_near, dr_near, dk_near, read_near, change_near, slope_ref, acc_ref,
    z_ref, d_ref, zx_ref, dx_decay, dc_ref, t_ref, rec_ref, q_ref, p_ref, y_ref, st_ref,
    wa_ref, wb_ref, wx_ref, wt_ref, wr_ref, ws_ref,
    swap_send, swap_recv, out_send, out_recv, back_send, back_recv, end_send, end_recv,
    give_send, give_recv, cast_send, cast_recv, share_send, share_recv, last_send, last_recv,
):
    seq = lax.axis_index("seq")
    chip, core = seq // 2, seq % 2
    other = 1 - core
    mine = lax.axis_index("dp") * CHIPS + chip
    partner = {"seq": chip * 2 + other}

    def peer(m):
        return {"seq": m * 2 + core}

    def owner(c):
        return {"seq": lax.rem(c, CHIPS) * 2 + core, "dp": c // CHIPS}

    def turn(o):
        return lax.rem(chip + o, CHIPS)

    def wide_turn(o):
        return lax.rem(mine + o, CHUNKS)

    fetches = [
        pltpu.make_async_copy(source, target, fetch_sem.at[i])
        for i, (source, target) in enumerate(
            (
                (x_hbm, x_ref),
                (a_hbm, a_ref),
                (b_hbm, b_ref),
                (k_hbm, k_ref),
                (r_hbm, r_ref),
                (v_hbm, v_ref),
                (g_hbm, g_ref),
            )
        )
    ]
    for fetch in fetches:
        fetch.start()

    barrier = pltpu.get_barrier_semaphore()
    pl.semaphore_signal(barrier, inc=1, device_id=partner)

    @pl.loop(1, CHUNKS)
    def _(o):
        pl.semaphore_signal(barrier, inc=1, device_id=owner(wide_turn(o)))

    row, col, same = grids()
    lower = as_matrix(same & (row >= col))
    ones = as_matrix((row < HALF) == (col < HALF))
    left = col < HALF
    early = row < HALF
    around = jnp.where(
        same & ~early & (col < row), 1.0, jnp.where(same & early & (col >= row), -1.0, 0.0)
    ).astype(BF16)

    fetches[0].wait()
    fetches[1].wait()
    smooth = jnp.tanh(dot(x_ref[...], a_ref[...], NN))
    smooth_ref[...] = smooth
    gate_ref[...] = smooth.astype(BF16)
    acc_ref[...] = jnp.zeros_like(acc_ref)
    wa_ref[:, 40:, :] = jnp.zeros((CHUNKS, 8, 128), F32)
    wb_ref[:, 40:, :] = jnp.zeros((CHUNKS, 8, 128), F32)

    def lanes(group, pair):
        return pl.ds(pl.multiple_of(group * WIDTH + pair * 128, 128), 128)

    def vector(ref, group, pair):
        return ref[lanes(group, pair)].reshape(1, 128)

    def by_head(x):
        zero = jnp.zeros_like(x)
        return jnp.concatenate([jnp.where(left, x, zero), jnp.where(left, zero, x)], axis=0)

    def outputs_of(group):
        for pair in range(PAIRS):
            at = lanes(group, pair)
            s0, s1, e0, e1 = (
                spread(ref[:, at], left) for ref in (s0_ref, s1_ref, e0_ref, e1_ref)
            )
            mixed_ref[:, at] = (
                mixed_near[:, at] + both(reached_ref[:, at], s0, s1, NT)
            ).astype(BF16)
            dv_ref[:, at] = (dv_near[:, at] + both(faded_ref[:, at], e0, e1, NT)).astype(BF16)

    def states_of(group):
        gate = gate_ref[...]
        for pair in range(PAIRS):
            at = lanes(group, pair)
            log_decay, inclusive, exclusive, total0, total1 = decay_sums(
                gate, b_ref[at, :], vector(speed_ref, group, pair), lower
            )
            entering = jnp.exp(exclusive)
            leaving = jnp.exp(jnp.where(early, total0, total1) - inclusive)
            reached = (r_ref[:, at].astype(F32) * entering).astype(BF16)
            faded = (k_ref[:, at].astype(F32) * leaving).astype(BF16)
            log_ref[:, at] = log_decay
            sum_ref[:, at] = inclusive
            enter_ref[:, at] = entering
            leave_ref[:, at] = leaving
            reached_ref[:, at] = reached
            faded_ref[:, at] = faded
            v16, g16 = v_ref[:, at], g_ref[:, at]
            own0 = packed(dot(v16[:HALF], faded[:HALF], TN), left)
            own1 = packed(dot(v16[HALF:], faded[HALF:], TN), left)
            pull0 = packed(dot(g16[:HALF], reached[:HALF], TN), left)
            pull1 = packed(dot(g16[HALF:], reached[HALF:], TN), left)
            end0, end1 = jnp.exp(total0), jnp.exp(total1)
            own_ref[:, at] = own0
            pull_ref[:, at] = pull1
            ends_ref[0:1, at] = end0
            ends_ref[1:2, at] = end1
            rows = slice(pair * 8, pair * 8 + 8)
            chunks = pl.ds(group * 8, 8)
            z_ref[0, chunks, rows, :] = (end1 * own0 + own1).reshape(8, 8, 128)
            z_ref[1, chunks, rows, :] = (end0 * pull1 + pull0).reshape(8, 8, 128)
            d_ref[group, pair : pair + 1, :] = jnp.exp(total0 + total1)
        d_ref[group, PAIRS:, :] = jnp.zeros((8 - PAIRS, 128), F32)

    def near_terms(group):
        wide_row = lax.broadcasted_iota(jnp.int32, (TOK, 2 * TOK), 0)
        wide_col = lax.broadcasted_iota(jnp.int32, (TOK, 2 * TOK), 1) % TOK
        wide_same = (wide_row < HALF) == (wide_col < HALF)
        beneath = wide_same & (wide_row > wide_col)
        above = wide_same & (wide_row < wide_col)
        zero = jnp.zeros((), F32)
        for pair in range(PAIRS):
            at = lanes(group, pair)
            inclusive = sum_ref[:, at]
            middle = jnp.where(
                early,
                inclusive[HALF // 2 - 1 : HALF // 2],
                inclusive[HALF + HALF // 2 - 1 : HALF + HALF // 2],
            )
            upward = jnp.exp(inclusive - log_ref[:, at] - middle)
            downward = jnp.exp(middle - inclusive)
            v16, g16 = v_ref[:, at], g_ref[:, at]
            r, k, v, g = (t[:, at].astype(F32) for t in (r_ref, k_ref, v_ref, g_ref))
            reward = vector(reward_ref, group, pair)
            up = (r * upward).astype(BF16)
            down = (k * downward).astype(BF16)
            v2, g2, up2, down2 = by_head(v16), by_head(g16), by_head(up), by_head(down)
            scores = jnp.where(beneath, dot(up, down2, NT), zero).astype(BF16)
            scores_t = jnp.where(above, dot(down, up2, NT), zero).astype(BF16)
            products = jnp.where(beneath, dot(g16, v2, NT), zero).astype(BF16)
            products_t = jnp.where(above, dot(v16, g2, NT), zero).astype(BF16)
            present = summed_over(r * reward * k, ones)
            agreement = summed_over(v * g, ones)
            mixed_near[:, at] = dot(scores, v2, NN) + present * v
            dv_near[:, at] = dot(scores_t, g2, NN) + present * g
            near_past = dot(products, down2, NN)
            near_later = dot(products_t, up2, NN)
            dr_near[:, at] = upward * near_past + reward * k * agreement
            dk_near[:, at] = downward * near_later + reward * r * agreement
            read = up.astype(F32) * near_past
            read_near[:, at] = read
            change_near[:, at] = down.astype(F32) * near_later - read
            chunk = CHIPS * (group // 2) + PAIRS * (group % 2) + pair
            wb_ref[chunk, 40:41, :] = jnp.sum(r * k * agreement, axis=0, keepdims=True)

    def far_terms(group):
        gate = gate_ref[...]
        for pair in range(PAIRS):
            at = lanes(group, pair)
            rows = slice(pair * 8, pair * 8 + 8)
            chunks = pl.ds(group * 8, 8)
            start0 = st_ref[0, chunks, rows, :].reshape(HALF, 128)
            end1 = st_ref[1, chunks, rows, :].reshape(HALF, 128)
            start1 = ends_ref[0:1, at] * start0 + own_ref[:, at]
            end0 = ends_ref[1:2, at] * end1 + pull_ref[:, at]
            lows = [t.astype(BF16) for t in (start0, start1, end0, end1)]
            for low_ref, low in zip((s0_ref, s1_ref, e0_ref, e1_ref), lows):
                low_ref[:, at] = low
            s0, s1, e0, e1 = (spread(t, left) for t in lows)
            coupling = jnp.where(
                early,
                jnp.sum(lows[2].astype(F32) * start1, axis=0, keepdims=True),
                jnp.sum(end0 * lows[1].astype(F32), axis=0, keepdims=True),
            )
            reached, faded = reached_ref[:, at], faded_ref[:, at]
            past = both(g_ref[:, at], s0, s1, NN)
            later = both(v_ref[:, at], e0, e1, NN)
            dr_ref[:, at] = (dr_near[:, at] + enter_ref[:, at] * past).astype(BF16)
            dk_ref[:, at] = (dk_near[:, at] + leave_ref[:, at] * later).astype(BF16)
            far_read = reached.astype(F32) * past
            read = read_near[:, at] + far_read
            change = change_near[:, at] + (faded.astype(F32) * later - far_read)
            slope = (coupling + summed_by(around, change, 2) - read) * log_ref[:, at]
            slope_ref[:, at] = slope.astype(BF16)
            chunk = CHIPS * (group // 2) + PAIRS * (group % 2) + pair
            wa_ref[chunk, 40:41, :] = jnp.sum(slope, axis=0, keepdims=True)
        wide = pl.ds(pl.multiple_of(group * WIDTH, 128), WIDTH)
        slopes = slope_ref[:, wide]
        acc_ref[...] += dot(slopes, b_ref[wide, :], NN)
        wb_ref[pl.ds(group * BATCH, BATCH), :40, :] = dot(slopes, gate, TN).reshape(BATCH, 40, 128)

    def swap(group):
        chunks = pl.ds(group * 8, 8)
        return pltpu.make_async_remote_copy(
            z_ref.at[other, chunks], zx_ref.at[chunks],
            swap_send.at[group], swap_recv.at[group], device_id=partner,
        )

    def swap_decay(group):
        return pltpu.make_async_remote_copy(
            d_ref.at[group], dx_decay.at[group],
            swap_send.at[GROUPS + group], swap_recv.at[GROUPS + group], device_id=partner,
        )

    for fetch in fetches[2:]:
        fetch.wait()

    @pl.loop(0, GROUPS)
    def _(group):
        states_of(group)

        @pl.when(group == 0)
        def _():
            pl.semaphore_wait(barrier, CHUNKS)

        swap_decay(group).start()
        swap(group).start()

    @pl.loop(0, GROUPS)
    def _(group):
        swap_decay(group).wait_recv()
        dc_ref[group] = d_ref[group] * dx_decay[group]
        swap(group).wait_recv()

    def out_copy(m, slot):
        return pltpu.make_async_remote_copy(
            t_ref.at[m], rec_ref.at[slot], out_send.at[m], out_recv.at[slot], device_id=peer(m)
        )

    def back_copy(n, slot):
        return pltpu.make_async_remote_copy(
            q_ref.at[n], p_ref.at[slot], back_send.at[n], back_recv.at[slot], device_id=peer(n)
        )

    def end_copy(m):
        return pltpu.make_async_remote_copy(
            y_ref.at[m], st_ref.at[core, m], end_send.at[m], end_recv.at[m], device_id=partner
        )

    def end_wait(m):
        pltpu.make_async_remote_copy(
            y_ref.at[m], st_ref.at[other, m], end_send.at[m], end_recv.at[m], device_id=partner
        ).wait_recv()

    def chip_total(m, target):
        group = m // 8
        for j in range(PAIRS):
            rows = slice(8 * j, 8 * j + 8)
            target[rows, :] = (
                dx_decay[group, j : j + 1, :] * z_ref[core, m, rows, :] + zx_ref[m, rows, :]
            )
        target[40:48, :] = dc_ref[group]

    def pick(j):
        return (2 + 3 * j + 3 * (j // 2) + 2 * (j // 3)) % 4

    def farthest(i):
        y = lax.rem(chip // 8 + pick((i // 4) % 4), 4)
        x = lax.rem((chip // 4) % 2 + 1 - i // 16, 2)
        z = lax.rem(chip % 4 + pick(i % 4), 4)
        return (y * 2 + x) * 4 + z

    @pl.loop(0, CHIPS - 1)
    def _(i):
        m = farthest(i)
        chip_total(m, t_ref.at[m])
        out_copy(m, chip).start()

    chip_total(chip, rec_ref.at[chip])

    @pl.loop(0, GROUPS - 1)
    def _(group):
        near_terms(group)

    def step(i, carry):
        n = core * (CHIPS - 1) + (1 - 2 * core) * i

        @pl.when(n != chip)
        def _():
            out_copy(n, n).wait_recv()

        after = []
        for j in range(PAIRS):
            rows = slice(8 * j, 8 * j + 8)
            q_ref[n, rows, :] = carry[j]
            after.append(rec_ref[n, 40 + j : 41 + j, :] * carry[j] + rec_ref[n, rows, :])

        @pl.when(n != chip)
        def _():
            back_copy(n, chip).start()

        return tuple(after)

    lax.fori_loop(0, CHIPS, step, tuple(jnp.zeros((8, 128), F32) for _ in range(PAIRS)))

    near_terms(GROUPS - 1)

    def finish(m, source):
        group = m // 8
        st_ref[core, m] = source[...]
        for j in range(PAIRS):
            rows = slice(8 * j, 8 * j + 8)
            y_ref[m, rows, :] = (
                d_ref[group, j : j + 1, :] * source[rows, :] + z_ref[core, m, rows, :]
            )
        end_copy(m).start()

    finish(chip, q_ref.at[chip])

    @pl.loop(1, CHIPS)
    def _(o):
        m = turn(o)
        back_copy(m, m).wait_recv()
        finish(m, p_ref.at[m])

    def give(w_ref, part):
        at = pl.ds(part * BATCH, BATCH)
        return pltpu.make_async_remote_copy(
            w_ref.at[at], wx_ref.at[at], give_send.at[part], give_recv.at[part], device_id=partner
        )

    def cast(c, slot):
        return pltpu.make_async_remote_copy(
            wt_ref.at[c], wr_ref.at[slot], cast_send.at[c], cast_recv.at[slot], device_id=owner(c)
        )

    def ship(w_ref, part):
        give(w_ref, part).wait_recv()

        @pl.loop(0, BATCH)
        def _(i):
            c = part * BATCH + lax.rem(mine + 1 + i, BATCH)
            wt_ref[c] = w_ref[c] + wx_ref[c]

            @pl.when(c != mine)
            def _():
                cast(c, mine).start()

    def rotated(i):
        return lax.rem(mine // BATCH + 1 + i, GROUPS)

    @pl.loop(0, GROUPS)
    def _(i):
        group = rotated(i)

        @pl.loop(group * 8, group * 8 + 8)
        def _(m):
            end_wait(m)

        far_terms(group)

        @pl.when(core == 0)
        def _():
            give(wb_ref, group).start()

        @pl.when((core == 1) & (i > 0))
        def _():
            ship(wb_ref, rotated(i - 1))

    smooth = smooth_ref[...]
    project = (acc_ref[...] * (1.0 - smooth * smooth)).astype(BF16)

    @pl.loop(0, GROUPS)
    def _(i):
        group = rotated(i)
        wide = pl.ds(pl.multiple_of(group * WIDTH, 128), WIDTH)
        wa_ref[pl.ds(group * BATCH, BATCH), :40, :] = dot(x_ref[:, wide], project, TN).reshape(
            BATCH, 40, 128
        )

        @pl.when(core == 1)
        def _():
            give(wa_ref, group).start()

    @pl.when(core == 1)
    def _():
        ship(wb_ref, rotated(GROUPS - 1))

    @pl.when(core == 0)
    def _():
        @pl.loop(0, GROUPS)
        def _(i):
            ship(wa_ref, rotated(i))

    @pl.loop(0, GROUPS)
    def _(group):
        wide = pl.ds(pl.multiple_of(group * WIDTH, 128), WIDTH)
        dx_ref[:, wide] = dot(project, a_ref[wide, :], NT).astype(BF16)
        outputs_of(group)

    def share(n):
        return pltpu.make_async_remote_copy(
            ws_ref, red_ref.at[core, chip], share_send.at[n], share_recv.at[chip], device_id=peer(n)
        )

    def share_wait(n):
        pltpu.make_async_remote_copy(
            ws_ref, red_ref.at[core, n], share_send.at[n], share_recv.at[n], device_id=peer(n)
        ).wait_recv()

    def last(n):
        return pltpu.make_async_remote_copy(
            red_ref.at[core, n], red_ref.at[core, n], last_send.at[n], last_recv.at[n],
            device_id=partner,
        )

    def last_wait(n):
        pltpu.make_async_remote_copy(
            red_ref.at[other, n], red_ref.at[other, n], last_send.at[n], last_recv.at[n],
            device_id=partner,
        ).wait_recv()

    def add(o, total):
        c = wide_turn(o)
        cast(c, c).wait_recv()
        return total + wr_ref[c]

    ws_ref[...] = lax.fori_loop(1, CHUNKS, add, wt_ref[mine])

    @pl.loop(0, CHIPS - 1)
    def _(i):
        share(farthest(i)).start()

    red_ref[core, chip] = ws_ref[...]
    last(chip).start()

    @pl.loop(1, CHIPS)
    def _(o):
        n = turn(o)
        share_wait(n)
        last(n).start()

    end_copy(chip).wait_send()

    @pl.loop(1, CHIPS)
    def _(o):
        m = turn(o)
        out_copy(m, chip).wait_send()
        back_copy(m, chip).wait_send()
        end_copy(m).wait_send()
        share(m).wait_send()

    @pl.loop(0, GROUPS)
    def _(group):
        swap(group).wait_send()
        swap_decay(group).wait_send()
        give(wb_ref, group).wait_send()

    @pl.loop(1, CHUNKS)
    def _(o):
        cast(wide_turn(o), mine).wait_send()

    @pl.loop(0, CHIPS)
    def _(o):
        n = turn(o)
        last_wait(n)
        last(n).wait_send()


def summed_over(x, ones):
    total = None
    for piece in split(x, 2):
        term = dot(piece, ones, NN)
        total = term if total is None else total + term
    return total


def whole_stage(x, a, r, k, v, g, b, speed, reward):
    vmem = pl.BlockSpec(memory_space=pltpu.VMEM)
    channels = x.shape[1]
    full = jax.ShapeDtypeStruct((TOK, channels), BF16)
    wide = pltpu.VMEM((TOK, channels), F32)
    short = pltpu.VMEM((TOK, channels), BF16)
    half = pltpu.VMEM((HALF, channels), F32)
    low = pltpu.VMEM((HALF, channels), BF16)
    matrix = pltpu.VMEM((channels, 128), BF16)
    square = pltpu.VMEM((TOK, 128), F32)
    state = pltpu.VMEM((32, 40, 128), F32)
    states = pltpu.VMEM((2, 32, 40, 128), F32)
    message = pltpu.VMEM((32, 48, 128), F32)
    decay = pltpu.VMEM((GROUPS, 8, 128), F32)
    sums = pltpu.VMEM((CHUNKS, 48, 128), F32)
    sems = pltpu.SemaphoreType.DMA
    return pl.pallas_call(
        whole_kernel,
        in_specs=[pl.BlockSpec(memory_space=pltpu.HBM)] * 7 + [vmem] * 2,
        out_specs=[vmem] * 6,
        out_shape=[full] * 5 + [jax.ShapeDtypeStruct((2, CHIPS, 48, 128), F32)],
        scratch_shapes=[short, matrix, short, short, short, short, matrix, sems((7,))]
        + [low] * 4
        + [square, pltpu.VMEM((TOK, 128), BF16)]
        + [wide] * 4
        + [short] * 2
        + [half, half, pltpu.VMEM((8, channels), F32)]
        + [wide] * 6
        + [short, square]
        + [states, decay, state, decay, decay, message, message, state, state, state, states]
        + [sums] * 5
        + [pltpu.VMEM((48, 128), F32)]
        + [sems((2 * GROUPS,))] * 2
        + [sems((CHIPS,))] * 6
        + [sems((GROUPS,))] * 2
        + [sems((CHUNKS,))] * 2
        + [sems((CHIPS,))] * 4,
        compiler_params=pltpu.CompilerParams(
            collective_id=0, has_side_effects=True, vmem_limit_bytes=50 * 1024 * 1024
        ),
        name="whole_stage",
    )(x, a, r, k, v, g, b, speed, reward)


def emit_kernel(*refs):
    sources, red_ref = refs[:5], refs[5]
    targets, sem = refs[6:13], refs[15]
    time_ref, bonus_ref = refs[13:15]
    parts = list(sources) + [red_ref.at[0, :, pl.ds(0, 40)], red_ref.at[1, :, pl.ds(0, 40)]]
    copies = [
        pltpu.make_async_copy(part, target, sem.at[i])
        for i, (part, target) in enumerate(zip(parts, targets))
    ]
    for copy in copies:
        copy.start()
    for i in range(10):
        time_ref[pl.ds(128 * i, 128)] = red_ref[0, i, 40:41, :].reshape(128)
        bonus_ref[pl.ds(128 * i, 128)] = red_ref[1, i, 40:41, :].reshape(128)
    for copy in copies:
        copy.wait()


def emit_stage(mixed, dr, dk, dv, dx, red):
    vmem = pl.BlockSpec(memory_space=pltpu.VMEM)
    hbm = pl.BlockSpec(memory_space=pltpu.HBM)
    full = jax.ShapeDtypeStruct(mixed.shape, BF16)
    return pl.pallas_call(
        emit_kernel,
        in_specs=[vmem] * 6,
        out_specs=[hbm] * 7 + [vmem] * 2,
        out_shape=[full] * 5
        + [jax.ShapeDtypeStruct((CHIPS, 40, 128), F32)] * 2
        + [jax.ShapeDtypeStruct((1280,), F32)] * 2,
        scratch_shapes=[pltpu.SemaphoreType.DMA((7,))],
        compiler_params=pltpu.CompilerParams(vmem_limit_bytes=8 * 1024 * 1024),
        name="emit_stage",
    )(mixed, dr, dk, dv, dx, red)


def per_device(r, k, v, x, g, lowering, raising, speed, reward):
    r, k, v, x, g = (t[0] for t in (r, k, v, x, g))
    outs = emit_stage(*whole_stage(x, lowering, r, k, v, g, raising, speed, reward))
    lora = tuple(t.reshape(1280, 128) for t in outs[5:7])
    return tuple(t[None] for t in outs[:5]) + lora + tuple(outs[7:])


def solution(mesh):
    tokens = P("dp", "seq", None)
    return jax.shard_map(
        per_device,
        mesh=mesh,
        in_specs=(tokens,) * 5 + (P(),) * 4,
        out_specs=(tokens,) * 5 + (P("dp", None),) * 2 + (P("dp"),) * 2,
        check_vma=False,
    )
```

profile of v0, /device:TPU:1, one launch (start us, length us, event | category | flops | bytes accessed | tf_op | source)
XLA Modules:
  0.0 95.4 jit_solution(10912234717152206350)
XLA Ops:
  0.6 0.0 copy-start.1
  0.7 1.1 %copy-done.1 = bf16[1,128,2560]{2,1,0:T(8,128)(2,1)S(1)} copy-done((bf16[1,128,2560]{2,1,0:T(8,128)(2,1)S(1)}, bf16[1,128,2560]{2,1,0:T(8,128)(2,1)}, u32[]{:S(2)}) %copy-start.1) | copy-done | bytes 655384
  1.7 0.0 copy-start.2
  1.7 0.7 copy-done.2
  2.4 0.0 copy-start.3
  2.4 0.7 copy-done.3
  3.1 88.0 %whole_stage.1 = (bf16[128,2560]{1,0:T(8,128)(2,1)S(1)}, bf16[128,2560]{1,0:T(8,128)(2,1)S(1)}, bf16[128,2560]{1,0:T(8,128)(2,1)S(1)}, bf16[128,2560]{1,0:T(8,12...) custom-call(bf16[128,2560]{1,0:T(8,128)(2,1)S(1)} %bitcast.12, bf16[2560,128]{1,0:T(8,128)(2,1)} %a_hbm.1, ...), custom_call_target="tpu_custom_call" | custom-call | tf_op jit(solution)/shard_map/whole_stage/pallas_call | solution.py:581
  91.2 0.0 copy-start
  91.2 1.4 %copy-done = f32[2,32,48,128]{3,2,1,0:T(8,128)S(1)} copy-done((f32[2,32,48,128]{3,2,1,0:T(8,128)S(1)}, f32[2,32,48,128]{3,2,1,0:T(8,128)}, u32[]{:S(2)}) %copy-start) | copy-done | bytes 1572888
  92.6 2.8 %emit_stage.1 = (bf16[128,2560]{1,0:T(8,128)(2,1)}, bf16[128,2560]{1,0:T(8,128)(2,1)}, bf16[128,2560]{1,0:T(8,128)(2,1)}, bf16[128,2560]{1,0:T(8,128)(2,1)}, bf1...) custom-call(bf16[128,2560]{1,0:T(8,128)(2,1)S(1)} %get-tuple-element, ...), custom_call_target="tpu_custom_call" | custom-call | tf_op jit(solution)/shard_map/emit_stage/pallas_call | solution.py:631
Async XLA Ops:
  0.6 1.1 %copy-start.1 = (bf16[1,128,2560]{2,1,0:T(8,128)(2,1)S(1)}, bf16[1,128,2560]{2,1,0:T(8,128)(2,1)}, u32[]{:S(2)}) copy-start(bf16[1,128,2560]{2,1,0:T(8,128)(2,1)} %param.12) | copy-start | bytes 1966084
  1.7 0.7 copy-start.2
  2.4 0.7 copy-start.3
  91.2 1.4 %copy-start = (f32[2,32,48,128]{3,2,1,0:T(8,128)S(1)}, f32[2,32,48,128]{3,2,1,0:T(8,128)}, u32[]{:S(2)}) copy-start(f32[2,32,48,128]{3,2,1,0:T(8,128)} %get-tuple-element.29.refs_5_) | copy-start | bytes 4718596
where the time goes:
time: 96.3 us; the launch traced here: 95.4 us
  Pallas kernels  90.8 us (94%)
  local copies, waits for them, and re-layouts  3.89 us (4%)
    pallas_call x1, Pallas kernels, whole_stage(): pl.pallas_call(whole_kernel, in_specs=[pl.BlockSpec(memory_space=pltpu.HB...  88 us
    unnamed x8, local copies, waits for them, and re-layouts  3.89 us
    pallas_call x1, Pallas kernels, emit_stage(): pl.pallas_call(emit_kernel, in_specs=[vmem] * 6, out_specs=[hbm] * 7 + [v...  2.79 us

commit v1 on v0

--- a/solution.py
+++ b/solution.py
@@ -82,9 +82,9 @@
 
 
 def whole_kernel(
-    x_hbm, a_hbm, r_hbm, k_hbm, v_hbm, g_hbm, b_hbm, speed_ref, reward_ref,
+    x_hbm, a_hbm, r_hbm, k_hbm, v_hbm, g_hbm, b_hbm, speed_hbm, reward_hbm,
     mixed_ref, dr_ref, dk_ref, dv_ref, dx_ref, red_ref,
-    x_ref, a_ref, r_ref, k_ref, v_ref, g_ref, b_ref, fetch_sem,
+    x_ref, a_ref, r_ref, k_ref, v_ref, g_ref, b_ref, speed_ref, reward_ref, fetch_sem,
     s0_ref, s1_ref, e0_ref, e1_ref,
     smooth_ref, gate_ref, log_ref, sum_ref, enter_ref, leave_ref, reached_ref, faded_ref,
     own_ref, pull_ref, ends_ref,
@@ -119,10 +119,12 @@
                 (x_hbm, x_ref),
                 (a_hbm, a_ref),
                 (b_hbm, b_ref),
+                (speed_hbm, speed_ref),
                 (k_hbm, k_ref),
                 (r_hbm, r_ref),
                 (v_hbm, v_ref),
                 (g_hbm, g_ref),
+                (reward_hbm, reward_ref),
             )
         )
     ]
@@ -571,6 +573,7 @@
     half = pltpu.VMEM((HALF, channels), F32)
     low = pltpu.VMEM((HALF, channels), BF16)
     matrix = pltpu.VMEM((channels, 128), BF16)
+    vector = pltpu.VMEM((channels,), F32)
     square = pltpu.VMEM((TOK, 128), F32)
     state = pltpu.VMEM((32, 40, 128), F32)
     states = pltpu.VMEM((2, 32, 40, 128), F32)
@@ -578,12 +581,16 @@
     decay = pltpu.VMEM((GROUPS, 8, 128), F32)
     sums = pltpu.VMEM((CHUNKS, 48, 128), F32)
     sems = pltpu.SemaphoreType.DMA
+    speed, reward = (pltpu.with_memory_space_constraint(t, pltpu.HBM) for t in (speed, reward))
+    x, a, r, k, v, g, b = (
+        pltpu.with_memory_space_constraint(t, pltpu.HBM) for t in (x, a, r, k, v, g, b)
+    )
     return pl.pallas_call(
         whole_kernel,
-        in_specs=[pl.BlockSpec(memory_space=pltpu.HBM)] * 7 + [vmem] * 2,
+        in_specs=[pl.BlockSpec(memory_space=pltpu.HBM)] * 9,
         out_specs=[vmem] * 6,
         out_shape=[full] * 5 + [jax.ShapeDtypeStruct((2, CHIPS, 48, 128), F32)],
-        scratch_shapes=[short, matrix, short, short, short, short, matrix, sems((7,))]
+        scratch_shapes=[short, matrix, short, short, short, short, matrix, vector, vector, sems((9,))]
         + [low] * 4
         + [square, pltpu.VMEM((TOK, 128), BF16)]
         + [wide] * 4
@@ -607,16 +614,24 @@
 
 
 def emit_kernel(*refs):
-    sources, red_ref = refs[:5], refs[5]
-    targets, sem = refs[6:13], refs[15]
-    time_ref, bonus_ref = refs[13:15]
-    parts = list(sources) + [red_ref.at[0, :, pl.ds(0, 40)], red_ref.at[1, :, pl.ds(0, 40)]]
+    sources, red_hbm = refs[:5], refs[5]
+    targets, weights = refs[6:11], refs[11:13]
+    time_ref, bonus_ref, red_ref, red_sem, sem = refs[13:]
+    fetches = [
+        pltpu.make_async_copy(red_hbm.at[i], red_ref.at[i], red_sem.at[i]) for i in range(2)
+    ]
     copies = [
-        pltpu.make_async_copy(part, target, sem.at[i])
-        for i, (part, target) in enumerate(zip(parts, targets))
+        pltpu.make_async_copy(source, target, sem.at[i])
+        for i, (source, target) in enumerate(zip(sources, targets))
     ]
-    for copy in copies:
+    for copy in fetches + copies:
         copy.start()
+    for i, (fetch, target) in enumerate(zip(fetches, weights)):
+        fetch.wait()
+        copies.append(
+            pltpu.make_async_copy(red_ref.at[i, :, pl.ds(0, 40)], target, sem.at[5 + i])
+        )
+        copies[-1].start()
     for i in range(10):
         time_ref[pl.ds(128 * i, 128)] = red_ref[0, i, 40:41, :].reshape(128)
         bonus_ref[pl.ds(128 * i, 128)] = red_ref[1, i, 40:41, :].reshape(128)
@@ -628,14 +643,19 @@
     vmem = pl.BlockSpec(memory_space=pltpu.VMEM)
     hbm = pl.BlockSpec(memory_space=pltpu.HBM)
     full = jax.ShapeDtypeStruct(mixed.shape, BF16)
+    red = pltpu.with_memory_space_constraint(red, pltpu.HBM)
     return pl.pallas_call(
         emit_kernel,
-        in_specs=[vmem] * 6,
+        in_specs=[vmem] * 5 + [hbm],
         out_specs=[hbm] * 7 + [vmem] * 2,
         out_shape=[full] * 5
         + [jax.ShapeDtypeStruct((CHIPS, 40, 128), F32)] * 2
         + [jax.ShapeDtypeStruct((1280,), F32)] * 2,
-        scratch_shapes=[pltpu.SemaphoreType.DMA((7,))],
+        scratch_shapes=[
+            pltpu.VMEM(red.shape, F32),
+            pltpu.SemaphoreType.DMA((2,)),
+            pltpu.SemaphoreType.DMA((7,)),
+        ],
         compiler_params=pltpu.CompilerParams(vmem_limit_bytes=8 * 1024 * 1024),
         name="emit_stage",
     )(mixed, dr, dk, dv, dx, red)

time: 96.3 us -> 93.6 us (0.972)
  local copies, waits for them, and re-layouts: 3.89 us -> 0 us
  Pallas kernels: 90.8 us -> 92.8 us
    unnamed x8 -> x0, local copies, waits for them, and re-layouts: 3.89 us -> none
    pallas_call x1, Pallas kernels: 2.79 us -> 4.02 us  [emit_stage(): pl.pallas_call(emit_kernel, in_specs=[vmem] * 5 + [hbm], out_specs=[hbm]...]
where the time goes in v1:
time: 93.6 us; the launch traced here: 93.4 us
  Pallas kernels  92.8 us (99%)
    pallas_call x1, Pallas kernels, whole_stage(): pl.pallas_call(whole_kernel, in_specs=[pl.BlockSpec(memory_space=pltpu.HB...  88.8 us
    pallas_call x1, Pallas kernels, emit_stage(): pl.pallas_call(emit_kernel, in_specs=[vmem] * 5 + [hbm], out_specs=[hbm]...  4.02 us

profile of v1, /device:TPU:1, one launch (start us, length us, event | category | flops | bytes accessed | tf_op | source)
XLA Modules:
  0.0 93.4 jit_solution(4752889509124838784)
XLA Ops:
  0.6 88.8 %whole_stage.1 = (bf16[128,2560]{1,0:T(8,128)(2,1)S(1)}, bf16[128,2560]{1,0:T(8,128)(2,1)S(1)}, bf16[128,2560]{1,0:T(8,128)(2,1)S(1)}, bf16[128,2560]{1,0:T(8,12...) custom-call(bf16[128,2560]{1,0:T(8,128)(2,1)} %bitcast.12, bf16[2560,128]{1,0:T(8,128)(2,1)} %a_hbm.1, ...), custom_call_target="tpu_custom_call" | custom-call | tf_op jit(solution)/shard_map/whole_stage/pallas_call | solution.py:588
  89.4 4.0 %emit_stage.1 = (bf16[128,2560]{1,0:T(8,128)(2,1)}, bf16[128,2560]{1,0:T(8,128)(2,1)}, bf16[128,2560]{1,0:T(8,128)(2,1)}, bf16[128,2560]{1,0:T(8,128)(2,1)}, bf1...) custom-call(bf16[128,2560]{1,0:T(8,128)(2,1)S(1)} %get-tuple-element, ...), custom_call_target="tpu_custom_call" | custom-call | tf_op jit(solution)/shard_map/emit_stage/pallas_call | solution.py:647

commit v2 on v1

--- a/solution.py
+++ b/solution.py
@@ -70,6 +70,10 @@
     return jnp.concatenate([dot(lhs[:HALF], first, dims), dot(lhs[HALF:], last, dims)], axis=0)
 
 
+def twofold(pieces, high, low):
+    return dot(pieces[0], high, NN) + dot(pieces[1], high, NN) + dot(pieces[0], low, NN)
+
+
 def packed(product, left):
     return jnp.where(left[:HALF], product[:HALF], product[HALF:])
 
@@ -88,16 +92,17 @@
     s0_ref, s1_ref, e0_ref, e1_ref,
     smooth_ref, gate_ref, log_ref, sum_ref, enter_ref, leave_ref, reached_ref, faded_ref,
     own_ref, pull_ref, ends_ref,
-    mixed_near, dv_near, dr_near, dk_near, read_near, change_near, slope_ref, acc_ref,
+    mixed_near, dv_near, dr_near, dk_near, read_near, change_near, acc_ref,
     z_ref, d_ref, zx_ref, dx_decay, dc_ref, t_ref, rec_ref, q_ref, p_ref, y_ref, st_ref,
     wa_ref, wb_ref, wx_ref, wt_ref, wr_ref, ws_ref,
-    swap_send, swap_recv, out_send, out_recv, back_send, back_recv, end_send, end_recv,
-    give_send, give_recv, cast_send, cast_recv, share_send, share_recv, last_send, last_recv,
+    swap_send, decay_send, out_send, back_send, end_send, give_send, cast_send, share_send,
+    last_send, last_recv, swap_recv, back_recv, end_recv, give_recv, cast_recv,
 ):
     seq = lax.axis_index("seq")
     chip, core = seq // 2, seq % 2
     other = 1 - core
-    mine = lax.axis_index("dp") * CHIPS + chip
+    half = lax.axis_index("dp") * CHIPS
+    mine = half + chip
     partner = {"seq": chip * 2 + other}
 
     def peer(m):
@@ -177,38 +182,47 @@
             ).astype(BF16)
             dv_ref[:, at] = (dv_near[:, at] + both(faded_ref[:, at], e0, e1, NT)).astype(BF16)
 
+    def group_lanes(group):
+        return pl.ds(pl.multiple_of(group * WIDTH, 128), WIDTH)
+
+    def pair_lanes(pair):
+        return slice(pair * 128, pair * 128 + 128)
+
     def states_of(group):
-        gate = gate_ref[...]
+        wide = group_lanes(group)
+        early_wide = lax.broadcasted_iota(jnp.int32, (TOK, WIDTH), 0) < HALF
+        log_decay, inclusive, exclusive, total0, total1 = decay_sums(
+            gate_ref[...], b_ref[wide, :], speed_ref[wide].reshape(1, WIDTH), lower
+        )
+        log_ref[:, wide] = log_decay
+        sum_ref[:, wide] = inclusive
+        entering = jnp.exp(exclusive)
+        leaving = jnp.exp(jnp.where(early_wide, total0, total1) - inclusive)
+        enter_ref[:, wide] = entering
+        leave_ref[:, wide] = leaving
+        reached = (r_ref[:, wide].astype(F32) * entering).astype(BF16)
+        faded = (k_ref[:, wide].astype(F32) * leaving).astype(BF16)
+        reached_ref[:, wide] = reached
+        faded_ref[:, wide] = faded
+        end0, end1 = jnp.exp(total0), jnp.exp(total1)
+        ends_ref[0:1, wide] = end0
+        ends_ref[1:2, wide] = end1
+        decay = jnp.exp(total0 + total1)
+        chunks = pl.ds(group * 8, 8)
         for pair in range(PAIRS):
-            at = lanes(group, pair)
-            log_decay, inclusive, exclusive, total0, total1 = decay_sums(
-                gate, b_ref[at, :], vector(speed_ref, group, pair), lower
-            )
-            entering = jnp.exp(exclusive)
-            leaving = jnp.exp(jnp.where(early, total0, total1) - inclusive)
-            reached = (r_ref[:, at].astype(F32) * entering).astype(BF16)
-            faded = (k_ref[:, at].astype(F32) * leaving).astype(BF16)
-            log_ref[:, at] = log_decay
-            sum_ref[:, at] = inclusive
-            enter_ref[:, at] = entering
-            leave_ref[:, at] = leaving
-            reached_ref[:, at] = reached
-            faded_ref[:, at] = faded
-            v16, g16 = v_ref[:, at], g_ref[:, at]
-            own0 = packed(dot(v16[:HALF], faded[:HALF], TN), left)
-            own1 = packed(dot(v16[HALF:], faded[HALF:], TN), left)
-            pull0 = packed(dot(g16[:HALF], reached[:HALF], TN), left)
-            pull1 = packed(dot(g16[HALF:], reached[HALF:], TN), left)
-            end0, end1 = jnp.exp(total0), jnp.exp(total1)
-            own_ref[:, at] = own0
-            pull_ref[:, at] = pull1
-            ends_ref[0:1, at] = end0
-            ends_ref[1:2, at] = end1
+            at = pair_lanes(pair)
+            here = lanes(group, pair)
+            v16, g16 = v_ref[:, here], g_ref[:, here]
+            own0 = packed(dot(v16[:HALF], faded[:HALF, at], TN), left)
+            own1 = packed(dot(v16[HALF:], faded[HALF:, at], TN), left)
+            pull0 = packed(dot(g16[:HALF], reached[:HALF, at], TN), left)
+            pull1 = packed(dot(g16[HALF:], reached[HALF:, at], TN), left)
+            own_ref[:, here] = own0
+            pull_ref[:, here] = pull1
             rows = slice(pair * 8, pair * 8 + 8)
-            chunks = pl.ds(group * 8, 8)
-            z_ref[0, chunks, rows, :] = (end1 * own0 + own1).reshape(8, 8, 128)
-            z_ref[1, chunks, rows, :] = (end0 * pull1 + pull0).reshape(8, 8, 128)
-            d_ref[group, pair : pair + 1, :] = jnp.exp(total0 + total1)
+            z_ref[0, chunks, rows, :] = (end1[:, at] * own0 + own1).reshape(8, 8, 128)
+            z_ref[1, chunks, rows, :] = (end0[:, at] * pull1 + pull0).reshape(8, 8, 128)
+            d_ref[group, pair : pair + 1, :] = decay[:, at]
         d_ref[group, PAIRS:, :] = jnp.zeros((8 - PAIRS, 128), F32)
 
     def near_terms(group):
@@ -231,74 +245,83 @@
             v16, g16 = v_ref[:, at], g_ref[:, at]
             r, k, v, g = (t[:, at].astype(F32) for t in (r_ref, k_ref, v_ref, g_ref))
             reward = vector(reward_ref, group, pair)
-            up = (r * upward).astype(BF16)
-            down = (k * downward).astype(BF16)
+            up, up_low = split(r * upward, 2)
+            down, down_low = split(k * downward, 2)
             v2, g2, up2, down2 = by_head(v16), by_head(g16), by_head(up), by_head(down)
             scores = jnp.where(beneath, dot(up, down2, NT), zero).astype(BF16)
             scores_t = jnp.where(above, dot(down, up2, NT), zero).astype(BF16)
-            products = jnp.where(beneath, dot(g16, v2, NT), zero).astype(BF16)
-            products_t = jnp.where(above, dot(v16, g2, NT), zero).astype(BF16)
+            products = split(jnp.where(beneath, dot(g16, v2, NT), zero), 2)
+            products_t = split(jnp.where(above, dot(v16, g2, NT), zero), 2)
             present = summed_over(r * reward * k, ones)
             agreement = summed_over(v * g, ones)
             mixed_near[:, at] = dot(scores, v2, NN) + present * v
             dv_near[:, at] = dot(scores_t, g2, NN) + present * g
-            near_past = dot(products, down2, NN)
-            near_later = dot(products_t, up2, NN)
+            near_past = twofold(products, down2, by_head(down_low))
+            near_later = twofold(products_t, up2, by_head(up_low))
             dr_near[:, at] = upward * near_past + reward * k * agreement
             dk_near[:, at] = downward * near_later + reward * r * agreement
-            read = up.astype(F32) * near_past
+            read = (up.astype(F32) + up_low.astype(F32)) * near_past
             read_near[:, at] = read
-            change_near[:, at] = down.astype(F32) * near_later - read
+            change_near[:, at] = (
+                down.astype(F32) + down_low.astype(F32)
+            ) * near_later - read
             chunk = CHIPS * (group // 2) + PAIRS * (group % 2) + pair
             wb_ref[chunk, 40:41, :] = jnp.sum(r * k * agreement, axis=0, keepdims=True)
 
     def far_terms(group):
-        gate = gate_ref[...]
+        wide = group_lanes(group)
+        chunks = pl.ds(group * 8, 8)
+        starts, ends = [], []
         for pair in range(PAIRS):
-            at = lanes(group, pair)
             rows = slice(pair * 8, pair * 8 + 8)
-            chunks = pl.ds(group * 8, 8)
-            start0 = st_ref[0, chunks, rows, :].reshape(HALF, 128)
-            end1 = st_ref[1, chunks, rows, :].reshape(HALF, 128)
-            start1 = ends_ref[0:1, at] * start0 + own_ref[:, at]
-            end0 = ends_ref[1:2, at] * end1 + pull_ref[:, at]
-            lows = [t.astype(BF16) for t in (start0, start1, end0, end1)]
-            for low_ref, low in zip((s0_ref, s1_ref, e0_ref, e1_ref), lows):
-                low_ref[:, at] = low
-            s0, s1, e0, e1 = (spread(t, left) for t in lows)
-            coupling = jnp.where(
-                early,
-                jnp.sum(lows[2].astype(F32) * start1, axis=0, keepdims=True),
-                jnp.sum(end0 * lows[1].astype(F32), axis=0, keepdims=True),
-            )
-            reached, faded = reached_ref[:, at], faded_ref[:, at]
-            past = both(g_ref[:, at], s0, s1, NN)
-            later = both(v_ref[:, at], e0, e1, NN)
-            dr_ref[:, at] = (dr_near[:, at] + enter_ref[:, at] * past).astype(BF16)
-            dk_ref[:, at] = (dk_near[:, at] + leave_ref[:, at] * later).astype(BF16)
-            far_read = reached.astype(F32) * past
-            read = read_near[:, at] + far_read
-            change = change_near[:, at] + (faded.astype(F32) * later - far_read)
-            slope = (coupling + summed_by(around, change, 2) - read) * log_ref[:, at]
-            slope_ref[:, at] = slope.astype(BF16)
-            chunk = CHIPS * (group // 2) + PAIRS * (group % 2) + pair
-            wa_ref[chunk, 40:41, :] = jnp.sum(slope, axis=0, keepdims=True)
-        wide = pl.ds(pl.multiple_of(group * WIDTH, 128), WIDTH)
-        slopes = slope_ref[:, wide]
+            starts.append(st_ref[0, chunks, rows, :].reshape(HALF, 128))
+            ends.append(st_ref[1, chunks, rows, :].reshape(HALF, 128))
+        start0, end1 = jnp.concatenate(starts, axis=1), jnp.concatenate(ends, axis=1)
+        start1 = ends_ref[0:1, wide] * start0 + own_ref[:, wide]
+        end0 = ends_ref[1:2, wide] * end1 + pull_ref[:, wide]
+        lows = [t.astype(BF16) for t in (start0, start1, end0, end1)]
+        for low_ref, low in zip((s0_ref, s1_ref, e0_ref, e1_ref), lows):
+            low_ref[:, wide] = low
+        pasts, laters = [], []
+        for pair in range(PAIRS):
+            at = pair_lanes(pair)
+            here = lanes(group, pair)
+            s0, s1, e0, e1 = (spread(t[:, at], left) for t in lows)
+            pasts.append(both(g_ref[:, here], s0, s1, NN))
+            laters.append(both(v_ref[:, here], e0, e1, NN))
+        past, later = jnp.concatenate(pasts, axis=1), jnp.concatenate(laters, axis=1)
+        far_read = reached_ref[:, wide].astype(F32) * past
+        change = change_near[:, wide] + (faded_ref[:, wide].astype(F32) * later - far_read)
+        total = summed_by(around, change, 2)
+        dr_ref[:, wide] = (dr_near[:, wide] + enter_ref[:, wide] * past).astype(BF16)
+        dk_ref[:, wide] = (dk_near[:, wide] + leave_ref[:, wide] * later).astype(BF16)
+        coupling = jnp.where(
+            lax.broadcasted_iota(jnp.int32, (TOK, WIDTH), 0) < HALF,
+            jnp.sum(lows[2].astype(F32) * start1, axis=0, keepdims=True),
+            jnp.sum(end0 * lows[1].astype(F32), axis=0, keepdims=True),
+        )
+        slope = (coupling + total - (read_near[:, wide] + far_read)) * log_ref[:, wide]
+        slopes = slope.astype(BF16)
         acc_ref[...] += dot(slopes, b_ref[wide, :], NN)
-        wb_ref[pl.ds(group * BATCH, BATCH), :40, :] = dot(slopes, gate, TN).reshape(BATCH, 40, 128)
+        wb_ref[pl.ds(group * BATCH, BATCH), :40, :] = dot(slopes, gate_ref[...], TN).reshape(
+            BATCH, 40, 128
+        )
+        slope_sum = jnp.sum(slope, axis=0, keepdims=True)
+        chunk = CHIPS * (group // 2) + PAIRS * (group % 2)
+        for pair in range(PAIRS):
+            wa_ref[chunk + pair, 40:41, :] = slope_sum[:, pair_lanes(pair)]
 
     def swap(group):
         chunks = pl.ds(group * 8, 8)
         return pltpu.make_async_remote_copy(
             z_ref.at[other, chunks], zx_ref.at[chunks],
-            swap_send.at[group], swap_recv.at[group], device_id=partner,
+            swap_send, swap_recv.at[group], device_id=partner,
         )
 
     def swap_decay(group):
         return pltpu.make_async_remote_copy(
             d_ref.at[group], dx_decay.at[group],
-            swap_send.at[GROUPS + group], swap_recv.at[GROUPS + group], device_id=partner,
+            decay_send, swap_recv.at[GROUPS + group], device_id=partner,
         )
 
     for fetch in fetches[2:]:
@@ -323,22 +346,24 @@
 
     def out_copy(m, slot):
         return pltpu.make_async_remote_copy(
-            t_ref.at[m], rec_ref.at[slot], out_send.at[m], out_recv.at[slot], device_id=peer(m)
+            t_ref.at[m], rec_ref.at[slot], out_send, cast_recv.at[half + slot], device_id=peer(m)
         )
 
     def back_copy(n, slot):
         return pltpu.make_async_remote_copy(
-            q_ref.at[n], p_ref.at[slot], back_send.at[n], back_recv.at[slot], device_id=peer(n)
+            q_ref.at[n], p_ref.at[slot], back_send, back_recv.at[slot], device_id=peer(n)
         )
 
     def end_copy(m):
         return pltpu.make_async_remote_copy(
-            y_ref.at[m], st_ref.at[core, m], end_send.at[m], end_recv.at[m], device_id=partner
-        )
-
-    def end_wait(m):
+            y_ref.at[m], st_ref.at[core, m], end_send, end_recv.at[m // 8], device_id=partner
+        )
+
+    def end_wait(group):
+        chunks = pl.ds(group * 8, 8)
         pltpu.make_async_remote_copy(
-            y_ref.at[m], st_ref.at[other, m], end_send.at[m], end_recv.at[m], device_id=partner
+            y_ref.at[chunks], st_ref.at[other, chunks], end_send, end_recv.at[group],
+            device_id=partner,
         ).wait_recv()
 
     def chip_total(m, target):
@@ -415,12 +440,12 @@
     def give(w_ref, part):
         at = pl.ds(part * BATCH, BATCH)
         return pltpu.make_async_remote_copy(
-            w_ref.at[at], wx_ref.at[at], give_send.at[part], give_recv.at[part], device_id=partner
+            w_ref.at[at], wx_ref.at[at], give_send, give_recv.at[part], device_id=partner
         )
 
     def cast(c, slot):
         return pltpu.make_async_remote_copy(
-            wt_ref.at[c], wr_ref.at[slot], cast_send.at[c], cast_recv.at[slot], device_id=owner(c)
+            wt_ref.at[c], wr_ref.at[slot], cast_send, cast_recv.at[slot], device_id=owner(c)
         )
 
     def ship(w_ref, part):
@@ -442,10 +467,7 @@
     def _(i):
         group = rotated(i)
 
-        @pl.loop(group * 8, group * 8 + 8)
-        def _(m):
-            end_wait(m)
-
+        end_wait(group)
         far_terms(group)
 
         @pl.when(core == 0)
@@ -489,25 +511,18 @@
 
     def share(n):
         return pltpu.make_async_remote_copy(
-            ws_ref, red_ref.at[core, chip], share_send.at[n], share_recv.at[chip], device_id=peer(n)
+            ws_ref, red_ref.at[core, chip], share_send, back_recv.at[chip], device_id=peer(n)
         )
 
     def share_wait(n):
         pltpu.make_async_remote_copy(
-            ws_ref, red_ref.at[core, n], share_send.at[n], share_recv.at[n], device_id=peer(n)
+            ws_ref, red_ref.at[core, n], share_send, back_recv.at[n], device_id=peer(n)
         ).wait_recv()
 
     def last(n):
         return pltpu.make_async_remote_copy(
-            red_ref.at[core, n], red_ref.at[core, n], last_send.at[n], last_recv.at[n],
-            device_id=partner,
-        )
-
-    def last_wait(n):
-        pltpu.make_async_remote_copy(
-            red_ref.at[other, n], red_ref.at[other, n], last_send.at[n], last_recv.at[n],
-            device_id=partner,
-        ).wait_recv()
+            red_ref.at[core, n], red_ref.at[core, n], last_send, last_recv, device_id=partner
+        )
 
     def add(o, total):
         c = wide_turn(o)
@@ -529,31 +544,21 @@
         share_wait(n)
         last(n).start()
 
-    end_copy(chip).wait_send()
-
-    @pl.loop(1, CHIPS)
-    def _(o):
-        m = turn(o)
-        out_copy(m, chip).wait_send()
-        back_copy(m, chip).wait_send()
-        end_copy(m).wait_send()
-        share(m).wait_send()
-
-    @pl.loop(0, GROUPS)
-    def _(group):
-        swap(group).wait_send()
-        swap_decay(group).wait_send()
-        give(wb_ref, group).wait_send()
-
-    @pl.loop(1, CHUNKS)
-    def _(o):
-        cast(wide_turn(o), mine).wait_send()
-
-    @pl.loop(0, CHIPS)
-    def _(o):
-        n = turn(o)
-        last_wait(n)
-        last(n).wait_send()
+    def sent(ref, sem):
+        pltpu.make_async_remote_copy(ref, ref, sem, last_recv, device_id=partner).wait_send()
+
+    sent(z_ref.at[other], swap_send)
+    sent(d_ref, decay_send)
+    sent(t_ref.at[pl.ds(0, CHIPS - 1)], out_send)
+    sent(q_ref.at[pl.ds(0, CHIPS - 1)], back_send)
+    sent(y_ref, end_send)
+    sent(wb_ref, give_send)
+    sent(wt_ref.at[pl.ds(0, CHUNKS - 1)], cast_send)
+    sent(red_ref.at[core, pl.ds(0, CHIPS - 1)], share_send)
+    sent(red_ref.at[core], last_send)
+    pltpu.make_async_remote_copy(
+        red_ref.at[other], red_ref.at[other], last_send, last_recv, device_id=partner
+    ).wait_recv()
 
 
 def summed_over(x, ones):
@@ -597,15 +602,12 @@
         + [short] * 2
         + [half, half, pltpu.VMEM((8, channels), F32)]
         + [wide] * 6
-        + [short, square]
+        + [square]
         + [states, decay, state, decay, decay, message, message, state, state, state, states]
         + [sums] * 5
         + [pltpu.VMEM((48, 128), F32)]
-        + [sems((2 * GROUPS,))] * 2
-        + [sems((CHIPS,))] * 6
-        + [sems((GROUPS,))] * 2
-        + [sems((CHUNKS,))] * 2
-        + [sems((CHIPS,))] * 4,
+        + [sems(())] * 10
+        + [sems((2 * GROUPS,)), sems((CHIPS,)), sems((GROUPS,)), sems((GROUPS,)), sems((CHUNKS,))],
         compiler_params=pltpu.CompilerParams(
             collective_id=0, has_side_effects=True, vmem_limit_bytes=50 * 1024 * 1024
         ),

time: 93.6 us -> 86.1 us (0.920)
  Pallas kernels: 92.8 us -> 85.2 us
    pallas_call x1, Pallas kernels: 88.8 us -> 81.2 us  [whole_stage(): pl.pallas_call(whole_kernel, in_specs=[pl.BlockSpec(memory_space=pltpu.HB...]
where the time goes in v2:
time: 86.1 us; the launch traced here: 85.9 us
  Pallas kernels  85.2 us (99%)
    pallas_call x1, Pallas kernels, whole_stage(): pl.pallas_call(whole_kernel, in_specs=[pl.BlockSpec(memory_space=pltpu.HB...  81.2 us
    pallas_call x1, Pallas kernels, emit_stage(): pl.pallas_call(emit_kernel, in_specs=[vmem] * 5 + [hbm], out_specs=[hbm]...  4.02 us

profile of v2, /device:TPU:1, one launch (start us, length us, event | category | flops | bytes accessed | tf_op | source)
XLA Modules:
  0.0 85.9 jit_solution(1275582719854062867)
XLA Ops:
  0.6 81.2 %whole_stage.1 = (bf16[128,2560]{1,0:T(8,128)(2,1)S(1)}, bf16[128,2560]{1,0:T(8,128)(2,1)S(1)}, bf16[128,2560]{1,0:T(8,128)(2,1)S(1)}, bf16[128,2560]{1,0:T(8,12...) custom-call(bf16[128,2560]{1,0:T(8,128)(2,1)} %bitcast.12, bf16[2560,128]{1,0:T(8,128)(2,1)} %a_hbm.1, ...), custom_call_target="tpu_custom_call" | custom-call | tf_op jit(solution)/shard_map/whole_stage/pallas_call | solution.py:593
  81.9 4.0 %emit_stage.1 = (bf16[128,2560]{1,0:T(8,128)(2,1)}, bf16[128,2560]{1,0:T(8,128)(2,1)}, bf16[128,2560]{1,0:T(8,128)(2,1)}, bf16[128,2560]{1,0:T(8,128)(2,1)}, bf1...) custom-call(bf16[128,2560]{1,0:T(8,128)(2,1)S(1)} %get-tuple-element, ...), custom_call_target="tpu_custom_call" | custom-call | tf_op jit(solution)/shard_map/emit_stage/pallas_call | solution.py:649

commit v3 on v2

--- a/solution.py
+++ b/solution.py
@@ -15,6 +15,11 @@
 CHIPS = 32
 CHUNKS = 2 * CHIPS
 BATCH = CHUNKS // GROUPS
+HOPS = (0, 1, 2, 1)
+OFFSETS = sorted(
+    ((y, x, z) for y in range(4) for x in range(2) for z in range(4) if y + x + z > 0),
+    key=lambda step: -(HOPS[step[0]] + 2 * step[1] + HOPS[step[2]]),
+)
 NN = (((1,), (0,)), ((), ()))
 NT = (((1,), (1,)), ((), ()))
 TN = (((0,), (0,)), ((), ()))
@@ -139,9 +144,19 @@
     barrier = pltpu.get_barrier_semaphore()
     pl.semaphore_signal(barrier, inc=1, device_id=partner)
 
-    @pl.loop(1, CHUNKS)
-    def _(o):
-        pl.semaphore_signal(barrier, inc=1, device_id=owner(wide_turn(o)))
+    depths = [lax.rem(chip // 8 + d, 4) for d in range(4)]
+    sides = [lax.rem(chip // 4 + d, 2) for d in range(2)]
+    levels = [lax.rem(chip + d, 4) for d in range(4)]
+    far_first = [(depths[y], (depths[y] * 2 + sides[x]) * 4 + levels[z]) for y, x, z in OFFSETS]
+
+    for replica in (1 - lax.axis_index("dp"), lax.axis_index("dp")):
+        for _, m in far_first:
+            pl.semaphore_signal(
+                barrier, inc=1, device_id={"seq": m * 2 + core, "dp": replica}
+            )
+    pl.semaphore_signal(
+        barrier, inc=1, device_id={"dp": 1 - lax.axis_index("dp")}
+    )
 
     row, col, same = grids()
     lower = as_matrix(same & (row >= col))
@@ -366,8 +381,7 @@
             device_id=partner,
         ).wait_recv()
 
-    def chip_total(m, target):
-        group = m // 8
+    def chip_total(m, group, target):
         for j in range(PAIRS):
             rows = slice(8 * j, 8 * j + 8)
             target[rows, :] = (
@@ -375,22 +389,11 @@
             )
         target[40:48, :] = dc_ref[group]
 
-    def pick(j):
-        return (2 + 3 * j + 3 * (j // 2) + 2 * (j // 3)) % 4
-
-    def farthest(i):
-        y = lax.rem(chip // 8 + pick((i // 4) % 4), 4)
-        x = lax.rem((chip // 4) % 2 + 1 - i // 16, 2)
-        z = lax.rem(chip % 4 + pick(i % 4), 4)
-        return (y * 2 + x) * 4 + z
-
-    @pl.loop(0, CHIPS - 1)
-    def _(i):
-        m = farthest(i)
-        chip_total(m, t_ref.at[m])
+    for depth, m in far_first:
+        chip_total(m, depth, t_ref.at[m])
         out_copy(m, chip).start()
 
-    chip_total(chip, rec_ref.at[chip])
+    chip_total(chip, depths[0], rec_ref.at[chip])
 
     @pl.loop(0, GROUPS - 1)
     def _(group):
@@ -531,9 +534,8 @@
 
     ws_ref[...] = lax.fori_loop(1, CHUNKS, add, wt_ref[mine])
 
-    @pl.loop(0, CHIPS - 1)
-    def _(i):
-        share(farthest(i)).start()
+    for _, m in far_first:
+        share(m).start()
 
     red_ref[core, chip] = ws_ref[...]
     last(chip).start()

time: 86.1 us -> 83.2 us (0.966)
  Pallas kernels: 85.2 us -> 82.4 us
    pallas_call x1, Pallas kernels: 81.2 us -> 78.4 us  [whole_stage(): pl.pallas_call(whole_kernel, in_specs=[pl.BlockSpec(memory_space=pltpu.HB...]
where the time goes in v3:
time: 83.2 us; the launch traced here: 83.1 us
  Pallas kernels  82.4 us (99%)
    pallas_call x1, Pallas kernels, whole_stage(): pl.pallas_call(whole_kernel, in_specs=[pl.BlockSpec(memory_space=pltpu.HB...  78.4 us
    pallas_call x1, Pallas kernels, emit_stage(): pl.pallas_call(emit_kernel, in_specs=[vmem] * 5 + [hbm], out_specs=[hbm]...  4.02 us

profile of v3, /device:TPU:1, one launch (start us, length us, event | category | flops | bytes accessed | tf_op | source)
XLA Modules:
  0.0 83.1 jit_solution(4275033200216816009)
XLA Ops:
  0.6 78.4 %whole_stage.1 = (bf16[128,2560]{1,0:T(8,128)(2,1)S(1)}, bf16[128,2560]{1,0:T(8,128)(2,1)S(1)}, bf16[128,2560]{1,0:T(8,128)(2,1)S(1)}, bf16[128,2560]{1,0:T(8,12...) custom-call(bf16[128,2560]{1,0:T(8,128)(2,1)} %bitcast.12, bf16[2560,128]{1,0:T(8,128)(2,1)} %a_hbm.1, ...), custom_call_target="tpu_custom_call" | custom-call | tf_op jit(solution)/shard_map/whole_stage/pallas_call | solution.py:595
  79.0 4.0 %emit_stage.1 = (bf16[128,2560]{1,0:T(8,128)(2,1)}, bf16[128,2560]{1,0:T(8,128)(2,1)}, bf16[128,2560]{1,0:T(8,128)(2,1)}, bf16[128,2560]{1,0:T(8,128)(2,1)}, bf1...) custom-call(bf16[128,2560]{1,0:T(8,128)(2,1)S(1)} %get-tuple-element, ...), custom_call_target="tpu_custom_call" | custom-call | tf_op jit(solution)/shard_map/emit_stage/pallas_call | solution.py:651

commit v4 on v3

--- a/solution.py
+++ b/solution.py
@@ -112,9 +112,6 @@
 
     def peer(m):
         return {"seq": m * 2 + core}
-
-    def owner(c):
-        return {"seq": lax.rem(c, CHIPS) * 2 + core, "dp": c // CHIPS}
 
     def turn(o):
         return lax.rem(chip + o, CHIPS)
@@ -395,7 +392,7 @@
 
     chip_total(chip, depths[0], rec_ref.at[chip])
 
-    @pl.loop(0, GROUPS - 1)
+    @pl.loop(0, GROUPS // 2)
     def _(group):
         near_terms(group)
 
@@ -420,7 +417,9 @@
 
     lax.fori_loop(0, CHIPS, step, tuple(jnp.zeros((8, 128), F32) for _ in range(PAIRS)))
 
-    near_terms(GROUPS - 1)
+    @pl.loop(GROUPS // 2, GROUPS)
+    def _(group):
+        near_terms(group)
 
     def finish(m, source):
         group = m // 8
@@ -446,22 +445,23 @@
             w_ref.at[at], wx_ref.at[at], give_send, give_recv.at[part], device_id=partner
         )
 
-    def cast(c, slot):
-        return pltpu.make_async_remote_copy(
-            wt_ref.at[c], wr_ref.at[slot], cast_send, cast_recv.at[slot], device_id=owner(c)
+    def cast(c, slot, target):
+        return pltpu.make_async_remote_copy(
+            wt_ref.at[c], wr_ref.at[slot], cast_send, cast_recv.at[slot], device_id=target
         )
 
     def ship(w_ref, part):
         give(w_ref, part).wait_recv()
-
-        @pl.loop(0, BATCH)
-        def _(i):
-            c = part * BATCH + lax.rem(mine + 1 + i, BATCH)
-            wt_ref[c] = w_ref[c] + wx_ref[c]
-
-            @pl.when(c != mine)
-            def _():
-                cast(c, mine).start()
+        batch = pl.ds(part * BATCH, BATCH)
+        wt_ref[batch] = w_ref[batch] + wx_ref[batch]
+        for i in range(BATCH):
+            inner = lax.rem(mine + 1 + i, BATCH)
+            target = {"seq": ((part % 2) * BATCH + inner) * 2 + core, "dp": part // 2}
+            copy = cast(part * BATCH + inner, mine, target)
+            if i < BATCH - 1:
+                copy.start()
+            else:
+                pl.when(part != mine // BATCH)(copy.start)
 
     def rotated(i):
         return lax.rem(mine // BATCH + 1 + i, GROUPS)
@@ -529,7 +529,7 @@
 
     def add(o, total):
         c = wide_turn(o)
-        cast(c, c).wait_recv()
+        cast(c, c, partner).wait_recv()
         return total + wr_ref[c]
 
     ws_ref[...] = lax.fori_loop(1, CHUNKS, add, wt_ref[mine])

time: 83.2 us -> 82.4 us (level)
    pallas_call x1, Pallas kernels: 78.4 us -> 77.5 us  [whole_stage(): pl.pallas_call(whole_kernel, in_specs=[pl.BlockSpec(memory_space=pltpu.HB...]
where the time goes in v4:
time: 82.4 us; the launch traced here: 82.2 us
  Pallas kernels  81.6 us (99%)
    pallas_call x1, Pallas kernels, whole_stage(): pl.pallas_call(whole_kernel, in_specs=[pl.BlockSpec(memory_space=pltpu.HB...  77.5 us
    pallas_call x1, Pallas kernels, emit_stage(): pl.pallas_call(emit_kernel, in_specs=[vmem] * 5 + [hbm], out_specs=[hbm]...  4.02 us

profile of v4, /device:TPU:1, one launch (start us, length us, event | category | flops | bytes accessed | tf_op | source)
XLA Modules:
  0.0 82.2 jit_solution(6885524471802598727)
XLA Ops:
  0.6 77.5 %whole_stage.1 = (bf16[128,2560]{1,0:T(8,128)(2,1)S(1)}, bf16[128,2560]{1,0:T(8,128)(2,1)S(1)}, bf16[128,2560]{1,0:T(8,128)(2,1)S(1)}, bf16[128,2560]{1,0:T(8,12...) custom-call(bf16[128,2560]{1,0:T(8,128)(2,1)} %bitcast.12, bf16[2560,128]{1,0:T(8,128)(2,1)} %a_hbm.1, ...), custom_call_target="tpu_custom_call" | custom-call | tf_op jit(solution)/shard_map/whole_stage/pallas_call | solution.py:595
  78.2 4.0 %emit_stage.1 = (bf16[128,2560]{1,0:T(8,128)(2,1)}, bf16[128,2560]{1,0:T(8,128)(2,1)}, bf16[128,2560]{1,0:T(8,128)(2,1)}, bf16[128,2560]{1,0:T(8,128)(2,1)}, bf1...) custom-call(bf16[128,2560]{1,0:T(8,128)(2,1)S(1)} %get-tuple-element, ...), custom_call_target="tpu_custom_call" | custom-call | tf_op jit(solution)/shard_map/emit_stage/pallas_call | solution.py:651

commit v5 on v4

--- a/solution.py
+++ b/solution.py
@@ -343,12 +343,17 @@
     def _(group):
         states_of(group)
 
-        @pl.when(group == 0)
+        @pl.when(group == 2)
         def _():
             pl.semaphore_wait(barrier, CHUNKS)
-
-        swap_decay(group).start()
-        swap(group).start()
+            for earlier in range(2):
+                swap_decay(earlier).start()
+                swap(earlier).start()
+
+        @pl.when(group >= 2)
+        def _():
+            swap_decay(group).start()
+            swap(group).start()
 
     @pl.loop(0, GROUPS)
     def _(group):

time: 82.4 us -> 80.4 us (0.976)
  Pallas kernels: 81.6 us -> 79.6 us
    pallas_call x1, Pallas kernels: 77.5 us -> 75.5 us  [whole_stage(): pl.pallas_call(whole_kernel, in_specs=[pl.BlockSpec(memory_space=pltpu.HB...]
where the time goes in v5:
time: 80.4 us; the launch traced here: 80.2 us
  Pallas kernels  79.6 us (99%)
    pallas_call x1, Pallas kernels, whole_stage(): pl.pallas_call(whole_kernel, in_specs=[pl.BlockSpec(memory_space=pltpu.HB...  75.5 us
    pallas_call x1, Pallas kernels, emit_stage(): pl.pallas_call(emit_kernel, in_specs=[vmem] * 5 + [hbm], out_specs=[hbm]...  4.02 us

profile of v5, /device:TPU:1, one launch (start us, length us, event | category | flops | bytes accessed | tf_op | source)
XLA Modules:
  0.0 80.2 jit_solution(17740048617741436086)
XLA Ops:
  0.6 75.5 %whole_stage.1 = (bf16[128,2560]{1,0:T(8,128)(2,1)S(1)}, bf16[128,2560]{1,0:T(8,128)(2,1)S(1)}, bf16[128,2560]{1,0:T(8,128)(2,1)S(1)}, bf16[128,2560]{1,0:T(8,12...) custom-call(bf16[128,2560]{1,0:T(8,128)(2,1)} %bitcast.12, bf16[2560,128]{1,0:T(8,128)(2,1)} %a_hbm.1, ...), custom_call_target="tpu_custom_call" | custom-call | tf_op jit(solution)/shard_map/whole_stage/pallas_call | solution.py:600
  76.2 4.0 %emit_stage.1 = (bf16[128,2560]{1,0:T(8,128)(2,1)}, bf16[128,2560]{1,0:T(8,128)(2,1)}, bf16[128,2560]{1,0:T(8,128)(2,1)}, bf16[128,2560]{1,0:T(8,128)(2,1)}, bf1...) custom-call(bf16[128,2560]{1,0:T(8,128)(2,1)S(1)} %get-tuple-element, ...), custom_call_target="tpu_custom_call" | custom-call | tf_op jit(solution)/shard_map/emit_stage/pallas_call | solution.py:656
